TPU v7x, 128 devices: a whole 4x4x4 slice. The times are simulated.
128 devices in a mesh: row: 8 (over y, core), col: 16 (over z, x).
Axes of the slice: x: 4, y: 4, z: 4, core: 2. Of those that a mesh axis runs over, the one named last changes fastest.
Arguments:
- features: bfloat16 [262144, 256], P(('row', 'col')), may hold values from -6 to 6
- hub_features: bfloat16 [2048, 256], P(('row', 'col')), may hold values from -6 to 6
- w_self: bfloat16 [256, 256], replicated, may hold values from -0.375 to 0.375
- w_neigh: bfloat16 [256, 256], replicated, may hold values from -0.375 to 0.375
- out_bias: float32 [256], replicated, may hold values from -4 to 4
- local_edges: int32 [262144, 4], P(('row', 'col')), may hold values from 0 to 2047
- hub_edges: int32 [262144, 2], P(('row', 'col')), may hold values from 0 to 2047
- remote_edges: int32 [262144, 4], P(('row', 'col')), may hold values from 0 to 2047
- send_rows: int32 [128, 2048], P(('row', 'col')), may hold values from 0 to 2047
- cotangent: bfloat16 [262144, 256], P(('row', 'col')), may hold values from -6 to 6
Outputs:
- activated: bfloat16 [262144, 256], P(('row', 'col'))
- grad_features: float32 [262144, 256], P(('row', 'col'))
- grad_hubs: float32 [2048, 256], P(('row', 'col'))
- grad_w_self: float32 [256, 256], replicated
- grad_w_neigh: float32 [256, 256], replicated
- grad_bias: float32 [256], replicated
All inputs are finite; a program needn't handle non-finite values.
Results may differ from a plain program's by a relative error of at most 0.0075.
Values may be sent and summed in bfloat16 or wider, within the bound.
A program may use at most 64 MiB of HBM per device.

v0:
```python
import functools

import jax
import jax.numpy as jnp
from jax import lax
from jax.experimental import pallas as pl
from jax.experimental.pallas import tpu as pltpu
from jax.sharding import PartitionSpec as P

MESH = pl.DeviceIdType.MESH
F32 = jnp.float32
BF16 = jnp.bfloat16
TILE = 256


def kernel(
    rows_n,
    cols_n,
    fanouts,
    x_ref,
    hub_ref,
    ws_ref,
    wn_ref,
    bias_ref,
    el_ref,
    eh_ref,
    er_ref,
    es_ref,
    cot_ref,
    act_ref,
    gf_ref,
    ghub_ref,
    gws_ref,
    gwn_ref,
    gb_ref,
    erow,
    ecol,
    c_hub,
    c_rem,
    t_hub,
    t_rem,
    blk,
    send1,
    recv1,
    hub_all,
    send2,
    recv2,
    gm,
    pair_out,
    pair_in,
    hub_own,
    hub_send,
    hub_recv,
    wpart,
    wpair,
    wfinal,
    wrecv,
    wown,
    wtot,
    bpart,
    bpair,
    brecv,
    s_send,
    s_hub,
    s_hubp,
    s_bnd,
    s_wpair,
    s_w,
    s_b,
    s_gb,
    s_gpair,
    s_ghub,
    s_wag,
    s_wagp,
):
    fl, fh, fr = fanouts
    fanout = fl + fh + fr
    nodes, width = x_ref.shape
    tiles = nodes // TILE
    bnd = send1.shape[1]
    row = lax.axis_index("row")
    col = lax.axis_index("col")
    core = lax.rem(row, 2)
    yy = row // 2
    me = row * cols_n + col
    partner = (row + 1 - 2 * core, col)
    chips = rows_n // 2 * cols_n
    total = rows_n * cols_n
    chip = yy * cols_n + col

    def each_chip(fn):
        def outer(i, c):
            def inner(j, cc):
                y2 = lax.rem(yy + i, rows_n // 2)
                c2 = lax.rem(col + j, cols_n)

                @pl.when((i + j) > 0)
                def _():
                    fn(y2, c2)

                return cc

            return lax.fori_loop(0, cols_n, inner, c)

        lax.fori_loop(0, rows_n // 2, outer, 0)

    def remote(src, dst, ssem, rsem, dev):
        return pltpu.make_async_remote_copy(
            src_ref=src, dst_ref=dst, send_sem=ssem, recv_sem=rsem, device_id=dev, device_id_type=MESH
        )

    def drain(ref, sem):
        pltpu.make_async_copy(ref, ref, sem).wait()

    barrier = pltpu.get_barrier_semaphore()

    def greet_row(i, c):
        def greet(j, cc):
            @pl.when((i + j) > 0)
            def _():
                pl.semaphore_signal(
                    barrier,
                    inc=1,
                    device_id=(lax.rem(row + i, rows_n), lax.rem(col + j, cols_n)),
                    device_id_type=MESH,
                )

            return cc

        return lax.fori_loop(0, cols_n, greet, c)

    lax.fori_loop(0, rows_n, greet_row, 0)

    erow[...] = jnp.concatenate(
        [
            el_ref[...].astype(F32),
            eh_ref[...].astype(F32),
            er_ref[...].astype(F32),
            es_ref[...].astype(F32),
            jnp.zeros((16 - fanout - 1, nodes), F32),
        ],
        axis=0,
    )
    ecol[...] = erow[...].T
    local = range(0, fl)
    hubs = range(fl, fl + fh)
    remotes = range(fl + fh, fanout)
    lists = range(fanout, fanout + 1)

    lane_id = lax.broadcasted_iota(jnp.int32, (TILE, TILE), 1).astype(F32).astype(BF16)
    sub_id = lax.broadcasted_iota(jnp.int32, (TILE, TILE), 0).astype(F32).astype(BF16)
    one = jnp.ones((TILE, TILE), BF16)
    zero = jnp.zeros((TILE, TILE), BF16)

    def build_col(dst, dst_row, nb, js):
        edges = ecol[pl.ds(nb * TILE, TILE), :]
        for t in range(tiles):
            shifted = (edges - float(TILE * t)).astype(BF16)
            acc = None
            for j in js:
                hit = jnp.where(shifted[:, j : j + 1] == lane_id, one, zero)
                acc = hit if acc is None else acc + hit
            dst[pl.ds(dst_row, TILE), pl.ds(t * TILE, TILE)] = acc

    def build_row(dst, dst_row, rb, js):
        base = (rb * TILE).astype(F32)
        for t in range(tiles):
            shifted = (erow[:, pl.ds(t * TILE, TILE)] - base).astype(BF16)
            acc = None
            for j in js:
                hit = jnp.where(shifted[j : j + 1, :] == sub_id, one, zero)
                acc = hit if acc is None else acc + hit
            dst[pl.ds(dst_row, TILE), pl.ds(t * TILE, TILE)] = acc

    def dot(a, b):
        return jnp.dot(a, b, preferred_element_type=F32)

    pl.semaphore_wait(barrier, total - 1)

    hub_all[pl.ds(me * bnd, bnd), :] = hub_ref[...]
    each_chip(
        lambda y2, c2: remote(
            hub_ref, hub_all.at[pl.ds(me * bnd, bnd)], s_send.at[0], s_hub, (y2 * 2 + core, c2)
        ).start()
    )

    def send_row(i, c, src, dst, ssem, rsem):
        r2 = lax.rem(row + i, rows_n)

        def one_dest(j, cc):
            c2 = lax.rem(col + j, cols_n)

            @pl.when((i + j) > 0)
            def _():
                remote(src.at[r2 * cols_n + c2], dst.at[me], ssem, rsem, (r2, c2)).start()

            return cc

        return lax.fori_loop(0, cols_n, one_dest, c)

    def pick(i, c):
        r2 = lax.rem(row + i, rows_n)
        build_col(blk, 0, r2, lists)
        picked = dot(blk[...], x_ref[...]).astype(BF16)
        send1[pl.ds(r2 * cols_n, cols_n)] = picked.reshape(cols_n, bnd, width)
        return send_row(i, c, send1, recv1, s_send.at[1], s_bnd)

    lax.fori_loop(0, rows_n, pick, 0)
    recv1[me] = send1[me]

    def local_part(nb, c):
        build_col(blk, 0, nb, local)
        gf_ref[pl.ds(nb * TILE, TILE), :] = dot(blk[...], x_ref[...])
        build_col(c_hub, nb * TILE, nb, hubs)
        return c

    lax.fori_loop(0, tiles, local_part, 0)

    drain(hub_all.at[pl.ds(0, (chips - 1) * bnd)], s_hub)
    for y2 in range(rows_n // 2):
        part = hub_all.at[pl.ds((y2 * 2 + core) * TILE, TILE)]
        remote(part, part, s_send.at[2], s_hubp, partner).start()

    def counts_part(nb, c):
        build_col(c_rem, nb * TILE, nb, remotes)
        build_row(t_rem, nb * TILE, nb, remotes)
        build_row(t_hub, nb * TILE, nb, hubs)
        return c

    lax.fori_loop(0, tiles, counts_part, 0)
    drain(hub_all.at[pl.ds(0, rows_n // 2 * TILE)], s_hubp)

    def hub_part(nb, c):
        rows = pl.ds(nb * TILE, TILE)
        gf_ref[rows, :] += dot(c_hub[rows, :], hub_all[...])
        return c

    lax.fori_loop(0, tiles, hub_part, 0)
    drain(recv1.at[pl.ds(0, total - 1)], s_bnd)

    wpart[...] = jnp.zeros_like(wpart)
    bpart[...] = jnp.zeros_like(bpart)
    ta = (((0,), (0,)), ((), ()))
    tb = (((1,), (1,)), ((), ()))

    def dense(nb, c):
        rows = pl.ds(nb * TILE, TILE)
        incoming = recv1[...].reshape(total * bnd, width)
        summed = gf_ref[rows, :] + dot(c_rem[rows, :], incoming)
        mean = (summed / float(fanout)).astype(BF16)
        x = x_ref[rows, :]
        pre = dot(x, ws_ref[...]) + dot(mean, wn_ref[...]) + bias_ref[...]
        sig = jax.nn.sigmoid(pre)
        act_ref[rows, :] = (pre * sig).astype(BF16)
        gp = (cot_ref[rows, :].astype(F32) * sig * (1.0 + pre * (1.0 - sig))).astype(BF16)
        wpart[0] += lax.dot_general(x, gp, ta, preferred_element_type=F32)
        wpart[1] += lax.dot_general(mean, gp, ta, preferred_element_type=F32)
        bpart[0:1, :] += jnp.sum(gp.astype(F32), axis=0, keepdims=True)
        gm[rows, :] = (
            lax.dot_general(gp, wn_ref[...], tb, preferred_element_type=F32) / float(fanout)
        ).astype(BF16)
        gf_ref[rows, :] = lax.dot_general(gp, ws_ref[...], tb, preferred_element_type=F32)
        return c

    lax.fori_loop(0, tiles, dense, 0)

    remote(wpart.at[1 - core], wpair, s_send.at[3], s_wpair.at[0], partner).start()
    remote(bpart, bpair, s_send.at[4], s_wpair.at[1], partner).start()

    def spread_block(i, c):
        r2 = lax.rem(row + i, rows_n)
        out = dot(t_rem[pl.ds(r2 * TILE, TILE), :], gm[...]).astype(BF16)
        send2[pl.ds(r2 * cols_n, cols_n)] = out.reshape(cols_n, bnd, width)
        return send_row(i, c, send2, recv2, s_send.at[5], s_gb)

    spread_block(0, 0)
    drain(wpair, s_wpair.at[0])
    drain(bpair, s_wpair.at[1])
    wfinal[...] = wpart[core] + wpair[...]
    brecv[chip] = bpart[0:1, :] + bpair[0:1, :]

    def send_weights(y2, c2):
        other = y2 * cols_n + c2
        remote(
            wfinal.at[pl.ds(other // 2 * 8, 8), pl.ds(lax.rem(other, 2) * 128, 128)],
            wrecv.at[chip],
            s_send.at[6],
            s_w,
            (y2 * 2 + core, c2),
        ).start()
        remote(brecv.at[chip], brecv.at[chip], s_send.at[7], s_b, (y2 * 2 + core, c2)).start()

    each_chip(send_weights)
    wrecv[chip] = wfinal[pl.ds(chip // 2 * 8, 8), pl.ds(pl.multiple_of(lax.rem(chip, 2) * 128, 128), 128)]
    lax.fori_loop(1, rows_n, spread_block, 0)
    recv2[me] = send2[me]

    def hub_other(y2, c):
        r2 = y2 * 2 + 1 - core
        pair_out[pl.ds(y2 * TILE, TILE), :] = dot(
            t_hub[pl.ds(r2 * TILE, TILE), :], gm[...]
        ).astype(BF16)
        return c

    lax.fori_loop(0, rows_n // 2, hub_other, 0)
    remote(pair_out, pair_in, s_send.at[8], s_gpair, partner).start()

    def hub_mine(y2, c):
        r2 = y2 * 2 + core
        hub_own[pl.ds(y2 * TILE, TILE), :] = dot(t_hub[pl.ds(r2 * TILE, TILE), :], gm[...])
        return c

    lax.fori_loop(0, rows_n // 2, hub_mine, 0)
    drain(pair_in, s_gpair)

    def hub_join(y2, c):
        rows = pl.ds(y2 * TILE, TILE)
        both = (hub_own[rows, :] + pair_in[rows, :].astype(F32)).astype(BF16)
        hub_send[pl.ds(y2 * cols_n, cols_n)] = both.reshape(cols_n, bnd, width)
        return c

    lax.fori_loop(0, rows_n // 2, hub_join, 0)
    each_chip(
        lambda y2, c2: remote(
            hub_send.at[y2 * cols_n + c2],
            hub_recv.at[chip],
            s_send.at[9],
            s_ghub,
            (y2 * 2 + core, c2),
        ).start()
    )
    hub_recv[chip] = hub_send[chip]

    drain(wrecv.at[pl.ds(0, chips - 1)], s_w)
    drain(brecv.at[pl.ds(0, chips - 1)], s_b)
    own_tile = (pl.ds(pl.multiple_of(chip // 2 * 8, 8), 8), pl.ds(pl.multiple_of(lax.rem(chip, 2) * 128, 128), 128))
    wown[...] = jnp.sum(wrecv[...], axis=0)
    each_chip(
        lambda y2, c2: remote(
            wown, wtot.at[core].at[own_tile], s_send.at[10], s_wag, (y2 * 2 + core, c2)
        ).start()
    )
    wtot[(core,) + own_tile] = wown[...]
    gb_ref[...] = jnp.sum(brecv[...], axis=0)

    def local_back(rb, c):
        build_row(blk, 0, rb, local)
        gf_ref[pl.ds(rb * TILE, TILE), :] += dot(blk[...], gm[...])
        return c

    lax.fori_loop(0, tiles, local_back, 0)
    drain(wrecv.at[pl.ds(0, chips - 1)], s_wag)
    remote(wtot.at[core], wtot.at[core], s_send.at[11], s_wagp, partner).start()

    def return_counts(rb, c):
        build_row(c_rem, rb * TILE, rb, lists)
        return c

    lax.fori_loop(0, tiles, return_counts, 0)
    drain(wtot.at[0], s_wagp)
    gws_ref[...] = wtot[0]
    gwn_ref[...] = wtot[1]
    drain(recv2.at[pl.ds(0, total - 1)], s_gb)

    def return_block(rb, c):
        rows = pl.ds(rb * TILE, TILE)
        gf_ref[rows, :] += dot(c_rem[rows, :], recv2[...].reshape(total * bnd, width))
        return c

    lax.fori_loop(0, tiles, return_block, 0)
    drain(hub_recv.at[pl.ds(0, chips - 1)], s_ghub)
    ghub_ref[...] = jnp.sum(hub_recv[...].astype(F32), axis=0)

    drain(hub_all.at[pl.ds(0, (chips - 1) * bnd)], s_send.at[0])
    drain(recv1.at[pl.ds(0, total - 1)], s_send.at[1])
    drain(pair_in, s_send.at[2])
    drain(wpair, s_send.at[3])
    drain(bpair, s_send.at[4])
    drain(recv1.at[pl.ds(0, total - 1)], s_send.at[5])
    drain(wrecv.at[pl.ds(0, chips - 1)], s_send.at[6])
    drain(brecv.at[pl.ds(0, chips - 1)], s_send.at[7])
    drain(pair_in, s_send.at[8])
    drain(hub_recv.at[pl.ds(0, chips - 1)], s_send.at[9])
    drain(wrecv.at[pl.ds(0, chips - 1)], s_send.at[10])
    drain(wpair, s_send.at[11])


def solution(mesh):
    rows_n, cols_n = mesh.shape["row"], mesh.shape["col"]

    def body(
        features,
        hub_features,
        w_self,
        w_neigh,
        out_bias,
        local_edges,
        hub_edges,
        remote_edges,
        send_rows,
        cotangent,
    ):
        nodes, width = features.shape
        hub_own = hub_features.shape[0]
        total = rows_n * cols_n
        chips = total // 2
        bnd = send_rows.shape[1] // total
        hubs = hub_own * total
        fanouts = (local_edges.shape[1], hub_edges.shape[1], remote_edges.shape[1])
        vmem = pl.BlockSpec(memory_space=pltpu.VMEM)
        dma = pltpu.SemaphoreType.DMA
        outs = pl.pallas_call(
            functools.partial(kernel, rows_n, cols_n, fanouts),
            out_shape=(
                jax.ShapeDtypeStruct((nodes, width), BF16),
                jax.ShapeDtypeStruct((nodes, width), F32),
                jax.ShapeDtypeStruct((hub_own, width), F32),
                jax.ShapeDtypeStruct((width, width), F32),
                jax.ShapeDtypeStruct((width, width), F32),
                jax.ShapeDtypeStruct((1, width), F32),
            ),
            in_specs=[vmem] * 10,
            out_specs=(vmem,) * 6,
            scratch_shapes=[
                pltpu.VMEM((16, nodes), F32),
                pltpu.VMEM((nodes, 16), F32),
                pltpu.VMEM((nodes, hubs), BF16),
                pltpu.VMEM((nodes, total * bnd), BF16),
                pltpu.VMEM((hubs, nodes), BF16),
                pltpu.VMEM((total * bnd, nodes), BF16),
                pltpu.VMEM((TILE, nodes), BF16),
                pltpu.VMEM((total, bnd, width), BF16),
                pltpu.VMEM((total, bnd, width), BF16),
                pltpu.VMEM((hubs, width), BF16),
                pltpu.VMEM((total, bnd, width), BF16),
                pltpu.VMEM((total, bnd, width), BF16),
                pltpu.VMEM((nodes, width), BF16),
                pltpu.VMEM((hubs // 2, width), BF16),
                pltpu.VMEM((hubs // 2, width), BF16),
                pltpu.VMEM((hubs // 2, width), F32),
                pltpu.VMEM((chips, hub_own, width), BF16),
                pltpu.VMEM((chips, hub_own, width), BF16),
                pltpu.VMEM((2, width, width), F32),
                pltpu.VMEM((width, width), F32),
                pltpu.VMEM((width, width), F32),
                pltpu.VMEM((chips, 8, 128), F32),
                pltpu.VMEM((8, 128), F32),
                pltpu.VMEM((2, width, width), F32),
                pltpu.VMEM((8, width), F32),
                pltpu.VMEM((8, width), F32),
                pltpu.VMEM((chips, 1, width), F32),
                dma((12,)),
                dma,
                dma,
                dma,
                dma((2,)),
                dma,
                dma,
                dma,
                dma,
                dma,
                dma,
                dma,
            ],
            compiler_params=pltpu.CompilerParams(
                collective_id=0, has_side_effects=True, vmem_limit_bytes=60 << 20
            ),
        )(
            features,
            hub_features,
            w_self,
            w_neigh,
            out_bias.reshape(1, width),
            local_edges.T,
            hub_edges.T,
            remote_edges.T,
            send_rows,
            cotangent,
        )
        activated, grad_features, grad_hubs, grad_w_self, grad_w_neigh, grad_bias = outs
        return activated, grad_features, grad_hubs, grad_w_self, grad_w_neigh, grad_bias.reshape(width)

    by_node = P(("row", "col"), None)
    return jax.shard_map(
        body,
        mesh=mesh,
        in_specs=(by_node, by_node, P(), P(), P(), by_node, by_node, by_node, by_node, by_node),
        out_specs=(by_node, by_node, by_node, P(), P(), P()),
        check_vma=False,
    )
```

profile of v0, /device:TPU:1, one launch (start us, length us, event | category | flops | bytes accessed | tf_op | source)
XLA Modules:
  0.0 96.8 jit_solution(11738235198522700531)
XLA Ops:
  0.6 89.8 %shard_map.145 = (bf16[2048,256]{1,0:T(8,128)(2,1)}, f32[2048,256]{1,0:T(8,128)}, f32[16,256]{1,0:T(8,128)}, f32[256,256]{1,0:T(8,128)}, f32[256,256]{1,0:T(8,128)}, /*index=5*/f32[1,256]{1,0:T(1,128)}) custom-call(bf16[2048,256]{1,0:T(8,128)(2,1)} %x_ref.1, bf16[16,256]{1,0:T(8,128)(2,1)} %hub_ref.1, bf16[256,256]{1,0:T(8,128)(2,1)} %ws_ref.1, ...), custom_call_target="tpu_custom_call" | custom-call | tf_op jit(solution)/shard_map/pallas_call | solution.py:412
  90.4 0.0 copy-start
  90.4 2.4 %copy.22 = bf16[2048,256]{1,0:T(8,128)(2,1)} copy(bf16[2048,256]{1,0:T(8,128)(2,1)} %get-tuple-element.24) | data formatting | bytes 2097152
  92.8 0.0 copy-done
  92.8 0.0 copy-start.3
  92.8 0.0 copy-start.2
  92.8 0.0 copy-start.1
  92.8 0.0 copy-start.4
  92.9 1.3 %copy.23 = f32[2048,256]{1,0:T(8,128)} copy(f32[2048,256]{1,0:T(8,128)S(1)} %copy-done) | data formatting | bytes 4194304
  94.2 0.0 copy-done.3
  94.2 0.6 copy.24
  94.8 0.0 copy-done.2
  94.8 0.7 copy.25
  95.5 0.0 copy-done.1
  95.5 0.7 copy.26
  96.2 0.0 copy-done.4
  96.2 0.6 copy.27
Async XLA Ops:
  90.4 2.4 %copy-start = (f32[2048,256]{1,0:T(8,128)S(1)}, f32[2048,256]{1,0:T(8,128)}, u32[]{:S(2)}) copy-start(f32[2048,256]{1,0:T(8,128)} %get-tuple-element.25) | copy-start | bytes 6291460
  92.8 1.3 %copy-start.3 = (f32[16,256]{1,0:T(8,128)S(1)}, f32[16,256]{1,0:T(8,128)}, u32[]{:S(2)}) copy-start(f32[16,256]{1,0:T(8,128)} %get-tuple-element.26) | copy-start | bytes 49156
  92.8 1.9 %copy-start.2 = (f32[256,256]{1,0:T(8,128)S(1)}, f32[256,256]{1,0:T(8,128)}, u32[]{:S(2)}) copy-start(f32[256,256]{1,0:T(8,128)} %get-tuple-element.27) | copy-start | bytes 786436
  92.8 2.7 %copy-start.1 = (f32[256,256]{1,0:T(8,128)S(1)}, f32[256,256]{1,0:T(8,128)}, u32[]{:S(2)}) copy-start(f32[256,256]{1,0:T(8,128)} %get-tuple-element.28) | copy-start | bytes 786436
  92.8 3.4 %copy-start.4 = (f32[1,256]{1,0:T(1,128)S(1)}, f32[1,256]{1,0:T(1,128)}, u32[]{:S(2)}) copy-start(f32[1,256]{1,0:T(1,128)} %get-tuple-element.17) | copy-start | bytes 3076
where the time goes:
time: 96.9 us; the launch traced here: 96.8 us
  Pallas kernels  89.8 us (93%)
  local copies, waits for them, and re-layouts  6.33 us (7%)
    pallas_call x1, Pallas kernels, body(): pl.pallas_call(functools.partial(kernel, rows_n, cols_n, fanouts), out_sh...  89.8 us
    unnamed x16, local copies, waits for them, and re-layouts  6.33 us

commit v1 on v0

--- a/solution.py
+++ b/solution.py
@@ -11,13 +11,14 @@
 F32 = jnp.float32
 BF16 = jnp.bfloat16
 TILE = 256
+BIG = 512
 
 
 def kernel(
     rows_n,
     cols_n,
     fanouts,
-    x_ref,
+    x_in,
     hub_ref,
     ws_ref,
     wn_ref,
@@ -26,18 +27,23 @@
     eh_ref,
     er_ref,
     es_ref,
-    cot_ref,
-    act_ref,
-    gf_ref,
+    cot_in,
+    act_out,
+    gf_out,
     ghub_ref,
     gws_ref,
     gwn_ref,
     gb_ref,
+    x_ref,
+    cot_ref,
+    act_ref,
+    gf_ref,
+    mean_ref,
+    gp_ref,
     erow,
     ecol,
     c_hub,
     c_rem,
-    t_hub,
     t_rem,
     blk,
     send1,
@@ -53,7 +59,7 @@
     hub_recv,
     wpart,
     wpair,
-    wfinal,
+    wsend,
     wrecv,
     wown,
     wtot,
@@ -72,10 +78,15 @@
     s_ghub,
     s_wag,
     s_wagp,
+    s_io,
 ):
     fl, fh, fr = fanouts
     fanout = fl + fh + fr
     nodes, width = x_ref.shape
+    x_copy = pltpu.make_async_copy(x_in, x_ref, s_io.at[0])
+    x_copy.start()
+    cot_copy = pltpu.make_async_copy(cot_in, cot_ref, s_io.at[1])
+    cot_copy.start()
     tiles = nodes // TILE
     bnd = send1.shape[1]
     row = lax.axis_index("row")
@@ -88,21 +99,22 @@
     total = rows_n * cols_n
     chip = yy * cols_n + col
 
+    def far(i):
+        return lax.rem(2 + 3 * i + 3 * (i // 2) + 2 * (i // 3), 4)
+
+    def far_col(j):
+        z2 = lax.rem(col // 4 + far(j // 4), 4)
+        return z2 * 4 + lax.rem(col + far(lax.rem(j, 4)), 4)
+
+    def far_row(i):
+        return lax.rem(yy + far(i // 2), 4) * 2 + lax.rem(core + 1 + i, 2)
+
     def each_chip(fn):
-        def outer(i, c):
-            def inner(j, cc):
-                y2 = lax.rem(yy + i, rows_n // 2)
-                c2 = lax.rem(col + j, cols_n)
-
-                @pl.when((i + j) > 0)
-                def _():
-                    fn(y2, c2)
-
-                return cc
-
-            return lax.fori_loop(0, cols_n, inner, c)
-
-        lax.fori_loop(0, rows_n // 2, outer, 0)
+        def one_chip(k, c):
+            fn(lax.rem(yy + far(k // cols_n), 4), far_col(lax.rem(k, cols_n)))
+            return c
+
+        lax.fori_loop(0, chips - 1, one_chip, 0)
 
     def remote(src, dst, ssem, rsem, dev):
         return pltpu.make_async_remote_copy(
@@ -114,22 +126,16 @@
 
     barrier = pltpu.get_barrier_semaphore()
 
-    def greet_row(i, c):
-        def greet(j, cc):
-            @pl.when((i + j) > 0)
-            def _():
-                pl.semaphore_signal(
-                    barrier,
-                    inc=1,
-                    device_id=(lax.rem(row + i, rows_n), lax.rem(col + j, cols_n)),
-                    device_id_type=MESH,
-                )
-
-            return cc
-
-        return lax.fori_loop(0, cols_n, greet, c)
-
-    lax.fori_loop(0, rows_n, greet_row, 0)
+    def greet(k, c):
+        pl.semaphore_signal(
+            barrier,
+            inc=1,
+            device_id=(far_row(k // cols_n), far_col(lax.rem(k, cols_n))),
+            device_id_type=MESH,
+        )
+        return c
+
+    lax.fori_loop(0, total - 1, greet, 0)
 
     erow[...] = jnp.concatenate(
         [
@@ -184,33 +190,36 @@
         ).start()
     )
 
-    def send_row(i, c, src, dst, ssem, rsem):
-        r2 = lax.rem(row + i, rows_n)
-
-        def one_dest(j, cc):
-            c2 = lax.rem(col + j, cols_n)
-
-            @pl.when((i + j) > 0)
-            def _():
-                remote(src.at[r2 * cols_n + c2], dst.at[me], ssem, rsem, (r2, c2)).start()
-
-            return cc
-
-        return lax.fori_loop(0, cols_n, one_dest, c)
-
-    def pick(i, c):
-        r2 = lax.rem(row + i, rows_n)
+    def send_row(i, count, src, dst, ssem, rsem):
+        r2 = far_row(i)
+
+        def one_dest(j, c):
+            c2 = far_col(j)
+            remote(src.at[r2 * cols_n + c2], dst.at[me], ssem, rsem, (r2, c2)).start()
+            return c
+
+        lax.fori_loop(0, count, one_dest, 0)
+
+    def pick(i):
+        r2 = far_row(i)
         build_col(blk, 0, r2, lists)
-        picked = dot(blk[...], x_ref[...]).astype(BF16)
+        picked = dot(blk[pl.ds(0, TILE), :], x_ref[...]).astype(BF16)
         send1[pl.ds(r2 * cols_n, cols_n)] = picked.reshape(cols_n, bnd, width)
-        return send_row(i, c, send1, recv1, s_send.at[1], s_bnd)
-
-    lax.fori_loop(0, rows_n, pick, 0)
+
+    def pick_and_send(i, c):
+        pick(i)
+        send_row(i, cols_n, send1, recv1, s_send.at[1], s_bnd)
+        return c
+
+    x_copy.wait()
+    lax.fori_loop(0, rows_n - 1, pick_and_send, 0)
+    pick(rows_n - 1)
+    send_row(rows_n - 1, cols_n - 1, send1, recv1, s_send.at[1], s_bnd)
     recv1[me] = send1[me]
 
     def local_part(nb, c):
         build_col(blk, 0, nb, local)
-        gf_ref[pl.ds(nb * TILE, TILE), :] = dot(blk[...], x_ref[...])
+        gf_ref[pl.ds(nb * TILE, TILE), :] = dot(blk[pl.ds(0, TILE), :], x_ref[...])
         build_col(c_hub, nb * TILE, nb, hubs)
         return c
 
@@ -224,81 +233,90 @@
     def counts_part(nb, c):
         build_col(c_rem, nb * TILE, nb, remotes)
         build_row(t_rem, nb * TILE, nb, remotes)
-        build_row(t_hub, nb * TILE, nb, hubs)
         return c
 
     lax.fori_loop(0, tiles, counts_part, 0)
     drain(hub_all.at[pl.ds(0, rows_n // 2 * TILE)], s_hubp)
 
     def hub_part(nb, c):
-        rows = pl.ds(nb * TILE, TILE)
+        rows = pl.ds(nb * BIG, BIG)
         gf_ref[rows, :] += dot(c_hub[rows, :], hub_all[...])
         return c
 
-    lax.fori_loop(0, tiles, hub_part, 0)
+    lax.fori_loop(0, nodes // BIG, hub_part, 0)
     drain(recv1.at[pl.ds(0, total - 1)], s_bnd)
 
-    wpart[...] = jnp.zeros_like(wpart)
-    bpart[...] = jnp.zeros_like(bpart)
     ta = (((0,), (0,)), ((), ()))
     tb = (((1,), (1,)), ((), ()))
+    cot_copy.wait()
 
     def dense(nb, c):
-        rows = pl.ds(nb * TILE, TILE)
+        rows = pl.ds(nb * BIG, BIG)
         incoming = recv1[...].reshape(total * bnd, width)
         summed = gf_ref[rows, :] + dot(c_rem[rows, :], incoming)
         mean = (summed / float(fanout)).astype(BF16)
-        x = x_ref[rows, :]
-        pre = dot(x, ws_ref[...]) + dot(mean, wn_ref[...]) + bias_ref[...]
+        mean_ref[rows, :] = mean
+        pre = dot(x_ref[rows, :], ws_ref[...]) + dot(mean, wn_ref[...]) + bias_ref[...]
         sig = jax.nn.sigmoid(pre)
         act_ref[rows, :] = (pre * sig).astype(BF16)
-        gp = (cot_ref[rows, :].astype(F32) * sig * (1.0 + pre * (1.0 - sig))).astype(BF16)
-        wpart[0] += lax.dot_general(x, gp, ta, preferred_element_type=F32)
-        wpart[1] += lax.dot_general(mean, gp, ta, preferred_element_type=F32)
-        bpart[0:1, :] += jnp.sum(gp.astype(F32), axis=0, keepdims=True)
+        gp_ref[rows, :] = (
+            cot_ref[rows, :].astype(F32) * sig * (1.0 + pre * (1.0 - sig))
+        ).astype(BF16)
+        return c
+
+    lax.fori_loop(0, nodes // BIG, dense, 0)
+    act_copy = pltpu.make_async_copy(act_ref, act_out, s_io.at[2])
+    act_copy.start()
+
+    def back_mean(nb, c):
+        rows = pl.ds(nb * BIG, BIG)
         gm[rows, :] = (
-            lax.dot_general(gp, wn_ref[...], tb, preferred_element_type=F32) / float(fanout)
+            lax.dot_general(gp_ref[rows, :], wn_ref[...], tb, preferred_element_type=F32) / float(fanout)
         ).astype(BF16)
-        gf_ref[rows, :] = lax.dot_general(gp, ws_ref[...], tb, preferred_element_type=F32)
-        return c
-
-    lax.fori_loop(0, tiles, dense, 0)
-
+        return c
+
+    lax.fori_loop(0, nodes // BIG, back_mean, 0)
+    wpart[0] = lax.dot_general(x_ref[...], gp_ref[...], ta, preferred_element_type=F32)
+    wpart[1] = lax.dot_general(mean_ref[...], gp_ref[...], ta, preferred_element_type=F32)
+    bpart[0:1, :] = jnp.sum(gp_ref[...].astype(F32), axis=0, keepdims=True)
     remote(wpart.at[1 - core], wpair, s_send.at[3], s_wpair.at[0], partner).start()
     remote(bpart, bpair, s_send.at[4], s_wpair.at[1], partner).start()
 
-    def spread_block(i, c):
-        r2 = lax.rem(row + i, rows_n)
+    def spread_block(i):
+        r2 = far_row(i)
         out = dot(t_rem[pl.ds(r2 * TILE, TILE), :], gm[...]).astype(BF16)
         send2[pl.ds(r2 * cols_n, cols_n)] = out.reshape(cols_n, bnd, width)
-        return send_row(i, c, send2, recv2, s_send.at[5], s_gb)
-
-    spread_block(0, 0)
+
+    def spread_and_send(i, c):
+        spread_block(i)
+        send_row(i, cols_n, send2, recv2, s_send.at[5], s_gb)
+        return c
+
+    spread_and_send(jnp.int32(0), 0)
     drain(wpair, s_wpair.at[0])
     drain(bpair, s_wpair.at[1])
-    wfinal[...] = wpart[core] + wpair[...]
+    both = wpart[core] + wpair[...]
+    for h in range(2):
+        wsend[pl.ds(h * (chips // 2), chips // 2)] = both[:, h * 128 : h * 128 + 128].astype(BF16).reshape(chips // 2, 8, 128)
     brecv[chip] = bpart[0:1, :] + bpair[0:1, :]
 
     def send_weights(y2, c2):
-        other = y2 * cols_n + c2
-        remote(
-            wfinal.at[pl.ds(other // 2 * 8, 8), pl.ds(lax.rem(other, 2) * 128, 128)],
-            wrecv.at[chip],
-            s_send.at[6],
-            s_w,
-            (y2 * 2 + core, c2),
-        ).start()
-        remote(brecv.at[chip], brecv.at[chip], s_send.at[7], s_b, (y2 * 2 + core, c2)).start()
+        dev = (y2 * 2 + core, c2)
+        remote(wsend.at[y2 * cols_n + c2], wrecv.at[chip], s_send.at[6], s_w, dev).start()
+        remote(brecv.at[chip], brecv.at[chip], s_send.at[7], s_b, dev).start()
 
     each_chip(send_weights)
-    wrecv[chip] = wfinal[pl.ds(chip // 2 * 8, 8), pl.ds(pl.multiple_of(lax.rem(chip, 2) * 128, 128), 128)]
-    lax.fori_loop(1, rows_n, spread_block, 0)
+    wrecv[chip] = wsend[chip]
+    lax.fori_loop(1, rows_n - 1, spread_and_send, 0)
+    spread_block(rows_n - 1)
+    send_row(rows_n - 1, cols_n - 1, send2, recv2, s_send.at[5], s_gb)
     recv2[me] = send2[me]
 
     def hub_other(y2, c):
         r2 = y2 * 2 + 1 - core
+        build_row(blk, 0, r2, hubs)
         pair_out[pl.ds(y2 * TILE, TILE), :] = dot(
-            t_hub[pl.ds(r2 * TILE, TILE), :], gm[...]
+            blk[pl.ds(0, TILE), :], gm[...]
         ).astype(BF16)
         return c
 
@@ -307,7 +325,8 @@
 
     def hub_mine(y2, c):
         r2 = y2 * 2 + core
-        hub_own[pl.ds(y2 * TILE, TILE), :] = dot(t_hub[pl.ds(r2 * TILE, TILE), :], gm[...])
+        build_row(blk, 0, r2, hubs)
+        hub_own[pl.ds(y2 * TILE, TILE), :] = dot(blk[pl.ds(0, TILE), :], gm[...])
         return c
 
     lax.fori_loop(0, rows_n // 2, hub_mine, 0)
@@ -333,19 +352,21 @@
 
     drain(wrecv.at[pl.ds(0, chips - 1)], s_w)
     drain(brecv.at[pl.ds(0, chips - 1)], s_b)
-    own_tile = (pl.ds(pl.multiple_of(chip // 2 * 8, 8), 8), pl.ds(pl.multiple_of(lax.rem(chip, 2) * 128, 128), 128))
-    wown[...] = jnp.sum(wrecv[...], axis=0)
+    wown[...] = jnp.sum(wrecv[...].astype(F32), axis=0).astype(BF16)
     each_chip(
         lambda y2, c2: remote(
-            wown, wtot.at[core].at[own_tile], s_send.at[10], s_wag, (y2 * 2 + core, c2)
+            wown, wtot.at[core, chip], s_send.at[10], s_wag, (y2 * 2 + core, c2)
         ).start()
     )
-    wtot[(core,) + own_tile] = wown[...]
+    wtot[core, chip] = wown[...]
     gb_ref[...] = jnp.sum(brecv[...], axis=0)
 
     def local_back(rb, c):
+        rows = pl.ds(rb * TILE, TILE)
         build_row(blk, 0, rb, local)
-        gf_ref[pl.ds(rb * TILE, TILE), :] += dot(blk[...], gm[...])
+        gf_ref[rows, :] = dot(blk[pl.ds(0, TILE), :], gm[...]) + lax.dot_general(
+            gp_ref[rows, :], ws_ref[...], tb, preferred_element_type=F32
+        )
         return c
 
     lax.fori_loop(0, tiles, local_back, 0)
@@ -358,16 +379,20 @@
 
     lax.fori_loop(0, tiles, return_counts, 0)
     drain(wtot.at[0], s_wagp)
-    gws_ref[...] = wtot[0]
-    gwn_ref[...] = wtot[1]
+    for h in range(2):
+        part = pl.ds(h * (chips // 2), chips // 2)
+        gws_ref[:, pl.ds(h * 128, 128)] = wtot[0, part].astype(F32).reshape(width, 128)
+        gwn_ref[:, pl.ds(h * 128, 128)] = wtot[1, part].astype(F32).reshape(width, 128)
     drain(recv2.at[pl.ds(0, total - 1)], s_gb)
 
     def return_block(rb, c):
-        rows = pl.ds(rb * TILE, TILE)
+        rows = pl.ds(rb * BIG, BIG)
         gf_ref[rows, :] += dot(c_rem[rows, :], recv2[...].reshape(total * bnd, width))
         return c
 
-    lax.fori_loop(0, tiles, return_block, 0)
+    lax.fori_loop(0, nodes // BIG, return_block, 0)
+    gf_copy = pltpu.make_async_copy(gf_ref, gf_out, s_io.at[3])
+    gf_copy.start()
     drain(hub_recv.at[pl.ds(0, chips - 1)], s_ghub)
     ghub_ref[...] = jnp.sum(hub_recv[...].astype(F32), axis=0)
 
@@ -382,7 +407,21 @@
     drain(pair_in, s_send.at[8])
     drain(hub_recv.at[pl.ds(0, chips - 1)], s_send.at[9])
     drain(wrecv.at[pl.ds(0, chips - 1)], s_send.at[10])
-    drain(wpair, s_send.at[11])
+    drain(wtot.at[0], s_send.at[11])
+    act_copy.wait()
+    gf_copy.wait()
+
+
+def write_out(*refs):
+    count = len(refs) // 2
+    sems = refs[-1]
+    copies = [
+        pltpu.make_async_copy(refs[k], refs[count + k], sems.at[k]) for k in range(count)
+    ]
+    for copy in copies:
+        copy.start()
+    for copy in copies:
+        copy.wait()
 
 
 def solution(mesh):
@@ -408,6 +447,7 @@
         hubs = hub_own * total
         fanouts = (local_edges.shape[1], hub_edges.shape[1], remote_edges.shape[1])
         vmem = pl.BlockSpec(memory_space=pltpu.VMEM)
+        hbm = pl.BlockSpec(memory_space=pl.ANY)
         dma = pltpu.SemaphoreType.DMA
         outs = pl.pallas_call(
             functools.partial(kernel, rows_n, cols_n, fanouts),
@@ -419,14 +459,19 @@
                 jax.ShapeDtypeStruct((width, width), F32),
                 jax.ShapeDtypeStruct((1, width), F32),
             ),
-            in_specs=[vmem] * 10,
-            out_specs=(vmem,) * 6,
+            in_specs=[hbm] + [vmem] * 8 + [hbm],
+            out_specs=(hbm, hbm) + (vmem,) * 4,
             scratch_shapes=[
+                pltpu.VMEM((nodes, width), BF16),
+                pltpu.VMEM((nodes, width), BF16),
+                pltpu.VMEM((nodes, width), BF16),
+                pltpu.VMEM((nodes, width), F32),
+                pltpu.VMEM((nodes, width), BF16),
+                pltpu.VMEM((nodes, width), BF16),
                 pltpu.VMEM((16, nodes), F32),
                 pltpu.VMEM((nodes, 16), F32),
                 pltpu.VMEM((nodes, hubs), BF16),
                 pltpu.VMEM((nodes, total * bnd), BF16),
-                pltpu.VMEM((hubs, nodes), BF16),
                 pltpu.VMEM((total * bnd, nodes), BF16),
                 pltpu.VMEM((TILE, nodes), BF16),
                 pltpu.VMEM((total, bnd, width), BF16),
@@ -442,10 +487,10 @@
                 pltpu.VMEM((chips, hub_own, width), BF16),
                 pltpu.VMEM((2, width, width), F32),
                 pltpu.VMEM((width, width), F32),
-                pltpu.VMEM((width, width), F32),
-                pltpu.VMEM((chips, 8, 128), F32),
-                pltpu.VMEM((8, 128), F32),
-                pltpu.VMEM((2, width, width), F32),
+                pltpu.VMEM((chips, 8, 128), BF16),
+                pltpu.VMEM((chips, 8, 128), BF16),
+                pltpu.VMEM((8, 128), BF16),
+                pltpu.VMEM((2, chips, 8, 128), BF16),
                 pltpu.VMEM((8, width), F32),
                 pltpu.VMEM((8, width), F32),
                 pltpu.VMEM((chips, 1, width), F32),
@@ -461,6 +506,7 @@
                 dma,
                 dma,
                 dma,
+                dma((4,)),
             ],
             compiler_params=pltpu.CompilerParams(
                 collective_id=0, has_side_effects=True, vmem_limit_bytes=60 << 20
@@ -477,6 +523,13 @@
             send_rows,
             cotangent,
         )
+        outs = pl.pallas_call(
+            write_out,
+            out_shape=tuple(jax.ShapeDtypeStruct(o.shape, o.dtype) for o in outs),
+            in_specs=[hbm] * len(outs),
+            out_specs=(hbm,) * len(outs),
+            scratch_shapes=[dma((len(outs),))],
+        )(*outs)
         activated, grad_features, grad_hubs, grad_w_self, grad_w_neigh, grad_bias = outs
         return activated, grad_features, grad_hubs, grad_w_self, grad_w_neigh, grad_bias.reshape(width)
 

time: 96.9 us -> 206 us (2.13)
  Pallas kernels: 89.8 us -> 205 us
  local copies, waits for them, and re-layouts: 6.33 us -> 0 us
    pallas_call x0 -> x1, Pallas kernels: none -> 113 us  [body(): pl.pallas_call(write_out, out_shape=tuple((jax.ShapeDtypeStruct(o.shape,...]
    unnamed x16 -> x0, local copies, waits for them, and re-layouts: 6.33 us -> none
    pallas_call x1, Pallas kernels: 89.8 us -> 92 us  [body(): pl.pallas_call(functools.partial(kernel, rows_n, cols_n, fanouts), out_sh...]
where the time goes in v1:
time: 206 us
  Pallas kernels  205 us (100%)
    pallas_call x1, Pallas kernels, body(): pl.pallas_call(write_out, out_shape=tuple((jax.ShapeDtypeStruct(o.shape,...  113 us
    pallas_call x1, Pallas kernels, body(): pl.pallas_call(functools.partial(kernel, rows_n, cols_n, fanouts), out_sh...  92 us

profile of v1, /device:TPU:1, one launch (start us, length us, event | category | flops | bytes accessed | tf_op | source)
XLA Modules:
  0.0 205.5 jit_solution(2854127328089111231)
XLA Ops:
  0.6 92.0 %shard_map.145 = (bf16[2048,256]{1,0:T(8,128)(2,1)}, f32[2048,256]{1,0:T(8,128)}, f32[16,256]{1,0:T(8,128)}, f32[256,256]{1,0:T(8,128)}, f32[256,256]{1,0:T(8,128)}, /*index=5*/f32[1,256]{1,0:T(1,128)}) custom-call(bf16[2048,256]{1,0:T(8,128)(2,1)} %x_in.1, bf16[16,256]{1,0:T(8,128)(2,1)} %hub_ref.1, bf16[256,256]{1,0:T(8,128)(2,1)} %ws_ref.1, ...), custom_call_target="tpu_custom_call" | custom-call | tf_op jit(solution)/shard_map/pallas_call | solution.py:452
  92.7 112.9 %shard_map.146 = (bf16[2048,256]{1,0:T(8,128)(2,1)}, f32[2048,256]{1,0:T(8,128)}, f32[16,256]{1,0:T(8,128)}, f32[256,256]{1,0:T(8,128)}, f32[256,256]{1,0:T(8,128)}, /*index=5*/f32[1,256]{1,0:T(1,128)}) custom-call(bf16[2048,256]{1,0:T(8,128)(2,1)} %get-tuple-element.18.refs_0_, f32[2048,256]{1,0:T(8,128)} %get-tuple-element.19.refs_1_, ...), custom_call_target="tpu_custom_call" | custom-call | tf_op jit(solution)/shard_map/pallas_call | solution.py:526

commit v2 on v1

v2 whole, which is shorter than its diff:
```python
import functools

import jax
import jax.numpy as jnp
from jax import lax
from jax.experimental import pallas as pl
from jax.experimental.pallas import tpu as pltpu
from jax.sharding import PartitionSpec as P

MESH = pl.DeviceIdType.MESH
F32 = jnp.float32
BF16 = jnp.bfloat16
TILE = 256
BIG = 512


def kernel(
    rows_n,
    cols_n,
    fanouts,
    x_in,
    hub_ref,
    ws_ref,
    wn_ref,
    bias_ref,
    el_ref,
    eh_ref,
    er_ref,
    es_ref,
    cot_in,
    act_out,
    gf_out,
    ghub_ref,
    gws_ref,
    gwn_ref,
    gb_ref,
    x_ref,
    cot_ref,
    act_ref,
    gf_ref,
    mean_ref,
    gp_ref,
    pre_ref,
    erow,
    t_loc,
    t_hub,
    t_rem,
    t_list,
    send1,
    recv1,
    hub_all,
    send2,
    recv2,
    gm,
    pair_out,
    pair_in,
    hub_own,
    hub_send,
    hub_recv,
    wpart,
    wpair,
    wsend,
    wrecv,
    wown,
    wtot,
    bpart,
    bpair,
    brecv,
    s_send,
    s_hub,
    s_hubp,
    s_bnd,
    s_wpair,
    s_w,
    s_b,
    s_gb,
    s_gpair,
    s_ghub,
    s_wag,
    s_wagp,
    s_io,
):
    fl, fh, fr = fanouts
    fanout = fl + fh + fr
    nodes, width = x_ref.shape
    x_copy = pltpu.make_async_copy(x_in, x_ref, s_io.at[0])
    x_copy.start()
    cot_copy = pltpu.make_async_copy(cot_in, cot_ref, s_io.at[1])
    cot_copy.start()
    tiles = nodes // TILE
    bnd = send1.shape[1]
    row = lax.axis_index("row")
    col = lax.axis_index("col")
    core = lax.rem(row, 2)
    yy = row // 2
    me = row * cols_n + col
    partner = (row + 1 - 2 * core, col)
    chips = rows_n // 2 * cols_n
    total = rows_n * cols_n
    chip = yy * cols_n + col

    def far(i):
        return lax.rem(2 + 3 * i + 3 * (i // 2) + 2 * (i // 3), 4)

    order = (2, 1, 3, 0)
    zs = [lax.rem(col // 4 + dz, 4) * 4 for dz in order]
    xs = [lax.rem(col + dx, 4) for dx in order]
    far_cols = [z2 + x2 for z2 in zs for x2 in xs]

    def far_row(i):
        return lax.rem(yy + far(i // 2), 4) * 2 + lax.rem(core + 1 + i, 2)

    def each_chip(fn):
        def one_row(i, c):
            y2 = lax.rem(yy + far(i), 4)
            for c2 in far_cols:
                fn(y2, c2)
            return c

        lax.fori_loop(0, rows_n // 2 - 1, one_row, 0)
        for c2 in far_cols[:-1]:
            fn(yy, c2)

    def remote(src, dst, ssem, rsem, dev):
        return pltpu.make_async_remote_copy(
            src_ref=src, dst_ref=dst, send_sem=ssem, recv_sem=rsem, device_id=dev, device_id_type=MESH
        )

    def drain(ref, sem):
        pltpu.make_async_copy(ref, ref, sem).wait()

    barrier = pltpu.get_barrier_semaphore()

    def greet(r2, c2):
        pl.semaphore_signal(barrier, inc=1, device_id=(r2, c2), device_id_type=MESH)

    def greet_row(i, c):
        r2 = far_row(i)
        for c2 in far_cols:
            greet(r2, c2)
        return c

    lax.fori_loop(0, rows_n - 1, greet_row, 0)
    for c2 in far_cols[:-1]:
        greet(row, c2)

    erow[...] = jnp.concatenate(
        [
            el_ref[...].astype(F32),
            eh_ref[...].astype(F32),
            er_ref[...].astype(F32),
            es_ref[...].astype(F32),
            jnp.zeros((16 - fanout - 1, nodes), F32),
        ],
        axis=0,
    )
    local = range(0, fl)
    hubs = range(fl, fl + fh)
    remotes = range(fl + fh, fanout)
    lists = range(fanout, fanout + 1)

    sub_id = lax.broadcasted_iota(jnp.int32, (TILE, TILE), 0).astype(F32).astype(BF16)
    one = jnp.ones((TILE, TILE), BF16)
    zero = jnp.zeros((TILE, TILE), BF16)

    def build(dst, js):
        def strip(rb, c):
            base = (rb * TILE).astype(F32)
            for t in range(tiles):
                shifted = (erow[:, pl.ds(t * TILE, TILE)] - base).astype(BF16)
                acc = None
                for j in js:
                    hit = jnp.where(shifted[j : j + 1, :] == sub_id, one, zero)
                    acc = hit if acc is None else acc + hit
                dst[pl.ds(rb * TILE, TILE), pl.ds(t * TILE, TILE)] = acc
            return c

        lax.fori_loop(0, tiles, strip, 0)

    def dot(a, b):
        return jnp.dot(a, b, preferred_element_type=F32)

    def dot_rows(a, b):
        return lax.dot_general(a, b, (((0,), (0,)), ((), ())), preferred_element_type=F32)

    def dot_cols(a, b):
        return lax.dot_general(a, b, (((1,), (1,)), ((), ())), preferred_element_type=F32)

    build(t_list, lists)

    pl.semaphore_wait(barrier, total - 1)

    hub_all[pl.ds(me * bnd, bnd), :] = hub_ref[...]
    each_chip(
        lambda y2, c2: remote(
            hub_ref, hub_all.at[pl.ds(me * bnd, bnd)], s_send.at[0], s_hub, (y2 * 2 + core, c2)
        ).start()
    )

    def send_row(i, count, src, dst, ssem, rsem):
        r2 = far_row(i)
        for c2 in far_cols[:count]:
            remote(src.at[r2 * cols_n + c2], dst.at[me], ssem, rsem, (r2, c2)).start()

    x_copy.wait()
    send1[...] = dot_rows(t_list[...], x_ref[...]).astype(BF16).reshape(total, bnd, width)

    def send_picked(i, c):
        send_row(i, cols_n, send1, recv1, s_send.at[1], s_bnd)
        return c

    lax.fori_loop(0, rows_n - 1, send_picked, 0)
    send_row(rows_n - 1, cols_n - 1, send1, recv1, s_send.at[1], s_bnd)
    recv1[me] = send1[me]

    build(t_loc, local)
    gf_ref[...] = dot_rows(t_loc[...], x_ref[...])
    pre_ref[...] = dot(x_ref[...], ws_ref[...]) + bias_ref[...]

    drain(hub_all.at[pl.ds(0, (chips - 1) * bnd)], s_hub)
    for y2 in range(rows_n // 2):
        part = hub_all.at[pl.ds((y2 * 2 + core) * TILE, TILE)]
        remote(part, part, s_send.at[2], s_hubp, partner).start()

    build(t_hub, hubs)
    build(t_rem, remotes)
    drain(hub_all.at[pl.ds(0, rows_n // 2 * TILE)], s_hubp)

    gf_ref[...] += dot_rows(t_hub[...], hub_all[...])
    drain(recv1.at[pl.ds(0, total - 1)], s_bnd)

    cot_copy.wait()
    gf_ref[...] += dot_rows(t_rem[...], recv1[...].reshape(total * bnd, width))

    def dense(nb, c):
        rows = pl.ds(nb * BIG, BIG)
        mean = (gf_ref[rows, :] / float(fanout)).astype(BF16)
        mean_ref[rows, :] = mean
        pre = pre_ref[rows, :] + dot(mean, wn_ref[...])
        sig = jax.nn.sigmoid(pre)
        act_ref[rows, :] = (pre * sig).astype(BF16)
        gp_ref[rows, :] = (
            cot_ref[rows, :].astype(F32) * sig * (1.0 + pre * (1.0 - sig))
        ).astype(BF16)
        return c

    lax.fori_loop(0, nodes // BIG, dense, 0)
    act_copy = pltpu.make_async_copy(act_ref, act_out, s_io.at[2])
    act_copy.start()

    gm[...] = (dot_cols(gp_ref[...], wn_ref[...]) / float(fanout)).astype(BF16)

    def spread_and_send(i, c):
        y2 = lax.rem(yy + far(i), 4)
        out = dot(t_rem[pl.ds(pl.multiple_of(y2 * BIG, BIG), BIG), :], gm[...]).astype(BF16)
        send2[pl.ds(y2 * 2 * cols_n, 2 * cols_n)] = out.reshape(2 * cols_n, bnd, width)
        return c

    def spread_step(i, c):
        spread_and_send(i, 0)
        send_row(2 * i, cols_n, send2, recv2, s_send.at[5], s_gb)
        send_row(2 * i + 1, cols_n, send2, recv2, s_send.at[5], s_gb)
        return c

    lax.fori_loop(0, rows_n // 2 - 1, spread_step, 0)
    spread_and_send(jnp.int32(rows_n // 2 - 1), 0)
    send_row(rows_n - 2, cols_n, send2, recv2, s_send.at[5], s_gb)
    send_row(rows_n - 1, cols_n - 1, send2, recv2, s_send.at[5], s_gb)
    recv2[me] = send2[me]

    wpart[0] = dot_rows(x_ref[...], gp_ref[...])
    wpart[1] = dot_rows(mean_ref[...], gp_ref[...])
    bpart[0:1, :] = jnp.sum(gp_ref[...].astype(F32), axis=0, keepdims=True)
    remote(wpart.at[1 - core], wpair, s_send.at[3], s_wpair.at[0], partner).start()
    remote(bpart, bpair, s_send.at[4], s_wpair.at[1], partner).start()

    hub_own[...] = dot(t_hub[...], gm[...])
    for y2 in range(rows_n // 2):
        pair_out[pl.ds(y2 * TILE, TILE), :] = hub_own[
            pl.ds(pl.multiple_of((y2 * 2 + 1 - core) * TILE, TILE), TILE), :
        ].astype(BF16)
    remote(pair_out, pair_in, s_send.at[8], s_gpair, partner).start()

    drain(wpair, s_wpair.at[0])
    drain(bpair, s_wpair.at[1])
    both = wpart[core] + wpair[...]
    for h in range(2):
        wsend[pl.ds(h * (chips // 2), chips // 2)] = (
            both[:, h * 128 : h * 128 + 128].astype(BF16).reshape(chips // 2, 8, 128)
        )
    brecv[chip] = bpart[0:1, :] + bpair[0:1, :]

    def send_weights(y2, c2):
        dev = (y2 * 2 + core, c2)
        remote(wsend.at[y2 * cols_n + c2], wrecv.at[chip], s_send.at[6], s_w, dev).start()
        remote(brecv.at[chip], brecv.at[chip], s_send.at[7], s_b, dev).start()

    each_chip(send_weights)
    wrecv[chip] = wsend[chip]
    drain(pair_in, s_gpair)

    def hub_join(y2, c):
        rows = pl.ds(y2 * TILE, TILE)
        mine = hub_own[pl.ds((y2 * 2 + core) * TILE, TILE), :]
        both = (mine + pair_in[rows, :].astype(F32)).astype(BF16)
        hub_send[pl.ds(y2 * cols_n, cols_n)] = both.reshape(cols_n, bnd, width)
        return c

    lax.fori_loop(0, rows_n // 2, hub_join, 0)
    each_chip(
        lambda y2, c2: remote(
            hub_send.at[y2 * cols_n + c2],
            hub_recv.at[chip],
            s_send.at[9],
            s_ghub,
            (y2 * 2 + core, c2),
        ).start()
    )
    hub_recv[chip] = hub_send[chip]

    gf_ref[...] = dot_cols(gp_ref[...], ws_ref[...])
    gf_ref[...] += dot(t_loc[...], gm[...])
    drain(wrecv.at[pl.ds(0, chips - 1)], s_w)
    drain(brecv.at[pl.ds(0, chips - 1)], s_b)
    wown[...] = jnp.sum(wrecv[...].astype(F32), axis=0).astype(BF16)
    each_chip(
        lambda y2, c2: remote(
            wown, wtot.at[core, chip], s_send.at[10], s_wag, (y2 * 2 + core, c2)
        ).start()
    )
    wtot[core, chip] = wown[...]
    gb_ref[...] = jnp.sum(brecv[...], axis=0)

    drain(recv2.at[pl.ds(0, total - 1)], s_gb)

    gf_ref[...] += dot(t_list[...], recv2[...].reshape(total * bnd, width))
    gf_copy = pltpu.make_async_copy(gf_ref, gf_out, s_io.at[3])
    gf_copy.start()
    drain(wrecv.at[pl.ds(0, chips - 1)], s_wag)
    remote(wtot.at[core], wtot.at[core], s_send.at[11], s_wagp, partner).start()

    drain(hub_recv.at[pl.ds(0, chips - 1)], s_ghub)
    ghub_ref[...] = jnp.sum(hub_recv[...].astype(F32), axis=0)

    drain(wtot.at[0], s_wagp)
    for h in range(2):
        part = pl.ds(h * (chips // 2), chips // 2)
        gws_ref[:, pl.ds(h * 128, 128)] = wtot[0, part].astype(F32).reshape(width, 128)
        gwn_ref[:, pl.ds(h * 128, 128)] = wtot[1, part].astype(F32).reshape(width, 128)
    drain(hub_all.at[pl.ds(0, (chips - 1) * bnd)], s_send.at[0])
    drain(recv1.at[pl.ds(0, total - 1)], s_send.at[1])
    drain(pair_in, s_send.at[2])
    drain(wpair, s_send.at[3])
    drain(bpair, s_send.at[4])
    drain(recv1.at[pl.ds(0, total - 1)], s_send.at[5])
    drain(wrecv.at[pl.ds(0, chips - 1)], s_send.at[6])
    drain(brecv.at[pl.ds(0, chips - 1)], s_send.at[7])
    drain(pair_in, s_send.at[8])
    drain(hub_recv.at[pl.ds(0, chips - 1)], s_send.at[9])
    drain(wrecv.at[pl.ds(0, chips - 1)], s_send.at[10])
    drain(wtot.at[0], s_send.at[11])
    act_copy.wait()
    gf_copy.wait()


def write_out(pieces, *refs):
    count = len(pieces)
    sources, results, held = refs[:count], refs[count : 2 * count], refs[2 * count : 3 * count]
    arrive, leave = refs[3 * count], refs[3 * count + 1]
    steps = []
    for k, parts in enumerate(pieces):
        size = sources[k].shape[0] // parts
        for p in range(parts):
            rows = pl.ds(p * size, size)
            n = len(steps)
            steps.append(
                (
                    pltpu.make_async_copy(sources[k].at[rows], held[k].at[rows], arrive.at[n]),
                    pltpu.make_async_copy(held[k].at[rows], results[k].at[rows], leave.at[n]),
                )
            )
    for inward, outward in steps:
        inward.start()
    for inward, outward in steps:
        inward.wait()
        outward.start()
    for inward, outward in steps:
        outward.wait()


def solution(mesh):
    rows_n, cols_n = mesh.shape["row"], mesh.shape["col"]

    def body(
        features,
        hub_features,
        w_self,
        w_neigh,
        out_bias,
        local_edges,
        hub_edges,
        remote_edges,
        send_rows,
        cotangent,
    ):
        nodes, width = features.shape
        hub_own = hub_features.shape[0]
        total = rows_n * cols_n
        chips = total // 2
        bnd = send_rows.shape[1] // total
        hubs = hub_own * total
        fanouts = (local_edges.shape[1], hub_edges.shape[1], remote_edges.shape[1])
        vmem = pl.BlockSpec(memory_space=pltpu.VMEM)
        hbm = pl.BlockSpec(memory_space=pl.ANY)
        dma = pltpu.SemaphoreType.DMA
        outs = pl.pallas_call(
            functools.partial(kernel, rows_n, cols_n, fanouts),
            out_shape=(
                jax.ShapeDtypeStruct((nodes, width), BF16),
                jax.ShapeDtypeStruct((nodes, width), F32),
                jax.ShapeDtypeStruct((hub_own, width), F32),
                jax.ShapeDtypeStruct((width, width), F32),
                jax.ShapeDtypeStruct((width, width), F32),
                jax.ShapeDtypeStruct((1, width), F32),
            ),
            in_specs=[hbm] + [vmem] * 8 + [hbm],
            out_specs=(hbm, hbm) + (vmem,) * 4,
            scratch_shapes=[
                pltpu.VMEM((nodes, width), BF16),
                pltpu.VMEM((nodes, width), BF16),
                pltpu.VMEM((nodes, width), BF16),
                pltpu.VMEM((nodes, width), F32),
                pltpu.VMEM((nodes, width), BF16),
                pltpu.VMEM((nodes, width), BF16),
                pltpu.VMEM((nodes, width), F32),
                pltpu.VMEM((16, nodes), F32),
                pltpu.VMEM((nodes, nodes), BF16),
                pltpu.VMEM((hubs, nodes), BF16),
                pltpu.VMEM((total * bnd, nodes), BF16),
                pltpu.VMEM((nodes, total * bnd), BF16),
                pltpu.VMEM((total, bnd, width), BF16),
                pltpu.VMEM((total, bnd, width), BF16),
                pltpu.VMEM((hubs, width), BF16),
                pltpu.VMEM((total, bnd, width), BF16),
                pltpu.VMEM((total, bnd, width), BF16),
                pltpu.VMEM((nodes, width), BF16),
                pltpu.VMEM((hubs // 2, width), BF16),
                pltpu.VMEM((hubs // 2, width), BF16),
                pltpu.VMEM((hubs, width), F32),
                pltpu.VMEM((chips, hub_own, width), BF16),
                pltpu.VMEM((chips, hub_own, width), BF16),
                pltpu.VMEM((2, width, width), F32),
                pltpu.VMEM((width, width), F32),
                pltpu.VMEM((chips, 8, 128), BF16),
                pltpu.VMEM((chips, 8, 128), BF16),
                pltpu.VMEM((8, 128), BF16),
                pltpu.VMEM((2, chips, 8, 128), BF16),
                pltpu.VMEM((8, width), F32),
                pltpu.VMEM((8, width), F32),
                pltpu.VMEM((chips, 1, width), F32),
                dma((12,)),
                dma,
                dma,
                dma,
                dma((2,)),
                dma,
                dma,
                dma,
                dma,
                dma,
                dma,
                dma,
                dma((4,)),
            ],
            compiler_params=pltpu.CompilerParams(
                collective_id=0, has_side_effects=True, vmem_limit_bytes=60 << 20
            ),
        )(
            features,
            hub_features,
            w_self,
            w_neigh,
            out_bias.reshape(1, width),
            local_edges.T,
            hub_edges.T,
            remote_edges.T,
            send_rows,
            cotangent,
        )
        pieces = (2, 4, 1, 1, 1, 1)
        outs = pl.pallas_call(
            functools.partial(write_out, pieces),
            out_shape=tuple(jax.ShapeDtypeStruct(o.shape, o.dtype) for o in outs),
            in_specs=[hbm] * len(outs),
            out_specs=(hbm,) * len(outs),
            scratch_shapes=[pltpu.VMEM(o.shape, o.dtype) for o in outs]
            + [dma((sum(pieces),)), dma((sum(pieces),))],
        )(*outs)
        activated, grad_features, grad_hubs, grad_w_self, grad_w_neigh, grad_bias = outs
        return activated, grad_features, grad_hubs, grad_w_self, grad_w_neigh, grad_bias.reshape(width)

    by_node = P(("row", "col"), None)
    return jax.shard_map(
        body,
        mesh=mesh,
        in_specs=(by_node, by_node, P(), P(), P(), by_node, by_node, by_node, by_node, by_node),
        out_specs=(by_node, by_node, by_node, P(), P(), P()),
        check_vma=False,
    )
```

time: 206 us -> 78.9 us (0.38)
  Pallas kernels: 205 us -> 77.9 us
    pallas_call x1, Pallas kernels: 113 us -> 3.05 us  [body(): pl.pallas_call(functools.partial(write_out, pieces), out_shape=tuple((jax...]
    pallas_call x1, Pallas kernels: 92 us -> 74.9 us  [body(): pl.pallas_call(functools.partial(kernel, rows_n, cols_n, fanouts), out_sh...]
where the time goes in v2:
time: 78.9 us; the launch traced here: 78.8 us
  Pallas kernels  77.9 us (99%)
  between operations  0.82 us (1%)
    pallas_call x1, Pallas kernels, body(): pl.pallas_call(functools.partial(kernel, rows_n, cols_n, fanouts), out_sh...  74.9 us
    pallas_call x1, Pallas kernels, body(): pl.pallas_call(functools.partial(write_out, pieces), out_shape=tuple((jax...  3.05 us

profile of v2, /device:TPU:1, one launch (start us, length us, event | category | flops | bytes accessed | tf_op | source)
XLA Modules:
  0.0 78.8 jit_solution(11716797476591919672)
XLA Ops:
  0.6 74.9 %shard_map.145 = (bf16[2048,256]{1,0:T(8,128)(2,1)}, f32[2048,256]{1,0:T(8,128)}, f32[16,256]{1,0:T(8,128)}, f32[256,256]{1,0:T(8,128)}, f32[256,256]{1,0:T(8,128)}, /*index=5*/f32[1,256]{1,0:T(1,128)}) custom-call(bf16[2048,256]{1,0:T(8,128)(2,1)} %x_in.1, bf16[16,256]{1,0:T(8,128)(2,1)} %hub_ref.1, bf16[256,256]{1,0:T(8,128)(2,1)} %ws_ref.1, ...), custom_call_target="tpu_custom_call" | custom-call | tf_op jit(solution)/shard_map/pallas_call | solution.py:416
  75.5 3.0 %shard_map.146 = (bf16[2048,256]{1,0:T(8,128)(2,1)}, f32[2048,256]{1,0:T(8,128)}, f32[16,256]{1,0:T(8,128)}, f32[256,256]{1,0:T(8,128)}, f32[256,256]{1,0:T(8,128)}, /*index=5*/f32[1,256]{1,0:T(1,128)}) custom-call(bf16[2048,256]{1,0:T(8,128)(2,1)} %get-tuple-element.18.refs_0_, f32[2048,256]{1,0:T(8,128)} %get-tuple-element.19.refs_1_, ...), custom_call_target="tpu_custom_call" | custom-call | tf_op jit(solution)/shard_map/pallas_call | solution.py:491

commit v3 on v2

--- a/solution.py
+++ b/solution.py
@@ -163,19 +163,40 @@
     one = jnp.ones((TILE, TILE), BF16)
     zero = jnp.zeros((TILE, TILE), BF16)
 
+    def strip(dst, rb, js):
+        base = (rb * TILE).astype(F32)
+        for t in range(tiles):
+            shifted = (erow[:, pl.ds(t * TILE, TILE)] - base).astype(BF16)
+            acc = None
+            for j in js:
+                hit = jnp.where(shifted[j : j + 1, :] == sub_id, one, zero)
+                acc = hit if acc is None else acc + hit
+            dst[pl.ds(rb * TILE, TILE), pl.ds(t * TILE, TILE)] = acc
+
     def build(dst, js):
-        def strip(rb, c):
-            base = (rb * TILE).astype(F32)
-            for t in range(tiles):
-                shifted = (erow[:, pl.ds(t * TILE, TILE)] - base).astype(BF16)
-                acc = None
-                for j in js:
-                    hit = jnp.where(shifted[j : j + 1, :] == sub_id, one, zero)
-                    acc = hit if acc is None else acc + hit
-                dst[pl.ds(rb * TILE, TILE), pl.ds(t * TILE, TILE)] = acc
+        def one_strip(rb, c):
+            strip(dst, rb, js)
             return c
 
-        lax.fori_loop(0, tiles, strip, 0)
+        lax.fori_loop(0, tiles, one_strip, 0)
+
+    def gather_sum(out, counts, table, js=None):
+        def step(kb, c):
+            if js is not None:
+                strip(counts, 2 * kb, js)
+                strip(counts, 2 * kb + 1, js)
+            rows = pl.ds(kb * BIG, BIG)
+            out[...] += dot_rows(counts[rows, :], table[rows, :])
+            return c
+
+        lax.fori_loop(0, nodes // BIG, step, 0)
+
+    def in_blocks(fn, size=BIG):
+        def step(nb, c):
+            fn(pl.ds(nb * size, size))
+            return c
+
+        lax.fori_loop(0, nodes // size, step, 0)
 
     def dot(a, b):
         return jnp.dot(a, b, preferred_element_type=F32)
@@ -187,6 +208,7 @@
         return lax.dot_general(a, b, (((1,), (1,)), ((), ())), preferred_element_type=F32)
 
     build(t_list, lists)
+    gf_ref[...] = jnp.zeros_like(gf_ref)
 
     pl.semaphore_wait(barrier, total - 1)
 
@@ -203,37 +225,51 @@
             remote(src.at[r2 * cols_n + c2], dst.at[me], ssem, rsem, (r2, c2)).start()
 
     x_copy.wait()
-    send1[...] = dot_rows(t_list[...], x_ref[...]).astype(BF16).reshape(total, bnd, width)
+    gather_sum(gf_ref, t_list, x_ref)
+    send1[...] = gf_ref[...].astype(BF16).reshape(total, bnd, width)
 
     def send_picked(i, c):
-        send_row(i, cols_n, send1, recv1, s_send.at[1], s_bnd)
+        send_row(i, cols_n, send1, recv1, s_send.at[1], s_bnd.at[i // 2])
         return c
 
     lax.fori_loop(0, rows_n - 1, send_picked, 0)
-    send_row(rows_n - 1, cols_n - 1, send1, recv1, s_send.at[1], s_bnd)
+    send_row(rows_n - 1, cols_n - 1, send1, recv1, s_send.at[1], s_bnd.at[rows_n // 2 - 1])
     recv1[me] = send1[me]
 
-    build(t_loc, local)
-    gf_ref[...] = dot_rows(t_loc[...], x_ref[...])
-    pre_ref[...] = dot(x_ref[...], ws_ref[...]) + bias_ref[...]
+    gf_ref[...] = jnp.zeros_like(gf_ref)
+    gather_sum(gf_ref, t_loc, x_ref, local)
+
+    def own_part(rows):
+        pre_ref[rows, :] = dot(x_ref[rows, :], ws_ref[...]) + bias_ref[...]
+
+    in_blocks(own_part)
 
     drain(hub_all.at[pl.ds(0, (chips - 1) * bnd)], s_hub)
     for y2 in range(rows_n // 2):
         part = hub_all.at[pl.ds((y2 * 2 + core) * TILE, TILE)]
         remote(part, part, s_send.at[2], s_hubp, partner).start()
 
-    build(t_hub, hubs)
     build(t_rem, remotes)
     drain(hub_all.at[pl.ds(0, rows_n // 2 * TILE)], s_hubp)
 
-    gf_ref[...] += dot_rows(t_hub[...], hub_all[...])
-    drain(recv1.at[pl.ds(0, total - 1)], s_bnd)
-
+    gather_sum(gf_ref, t_hub, hub_all, hubs)
+
+    def remote_part(i):
+        y2 = lax.rem(yy + 4 - far(i), 4)
+        incoming = recv1[pl.ds(y2 * 2 * cols_n, 2 * cols_n)].reshape(BIG, width)
+        gf_ref[...] += dot_rows(t_rem[pl.ds(pl.multiple_of(y2 * BIG, BIG), BIG), :], incoming)
+
+    def remote_step(i, c):
+        drain(recv1.at[pl.ds(0, 2 * cols_n)], s_bnd.at[i])
+        remote_part(i)
+        return c
+
+    lax.fori_loop(0, rows_n // 2 - 1, remote_step, 0)
+    drain(recv1.at[pl.ds(0, 2 * cols_n - 1)], s_bnd.at[rows_n // 2 - 1])
     cot_copy.wait()
-    gf_ref[...] += dot_rows(t_rem[...], recv1[...].reshape(total * bnd, width))
-
-    def dense(nb, c):
-        rows = pl.ds(nb * BIG, BIG)
+    remote_part(jnp.int32(rows_n // 2 - 1))
+
+    def dense(rows):
         mean = (gf_ref[rows, :] / float(fanout)).astype(BF16)
         mean_ref[rows, :] = mean
         pre = pre_ref[rows, :] + dot(mean, wn_ref[...])
@@ -242,13 +278,16 @@
         gp_ref[rows, :] = (
             cot_ref[rows, :].astype(F32) * sig * (1.0 + pre * (1.0 - sig))
         ).astype(BF16)
-        return c
-
-    lax.fori_loop(0, nodes // BIG, dense, 0)
+
+    in_blocks(dense)
     act_copy = pltpu.make_async_copy(act_ref, act_out, s_io.at[2])
     act_copy.start()
 
-    gm[...] = (dot_cols(gp_ref[...], wn_ref[...]) / float(fanout)).astype(BF16)
+
+    def back_mean(rows):
+        gm[rows, :] = (dot_cols(gp_ref[rows, :], wn_ref[...]) / float(fanout)).astype(BF16)
+
+    in_blocks(back_mean)
 
     def spread_and_send(i, c):
         y2 = lax.rem(yy + far(i), 4)
@@ -268,13 +307,23 @@
     send_row(rows_n - 1, cols_n - 1, send2, recv2, s_send.at[5], s_gb)
     recv2[me] = send2[me]
 
-    wpart[0] = dot_rows(x_ref[...], gp_ref[...])
-    wpart[1] = dot_rows(mean_ref[...], gp_ref[...])
-    bpart[0:1, :] = jnp.sum(gp_ref[...].astype(F32), axis=0, keepdims=True)
+    wpart[...] = jnp.zeros_like(wpart)
+    bpart[...] = jnp.zeros_like(bpart)
+
+    def weight_part(rows):
+        gp = gp_ref[rows, :]
+        wpart[0] += dot_rows(x_ref[rows, :], gp)
+        wpart[1] += dot_rows(mean_ref[rows, :], gp)
+        bpart[0:1, :] += jnp.sum(gp.astype(F32), axis=0, keepdims=True)
+
+    in_blocks(weight_part)
     remote(wpart.at[1 - core], wpair, s_send.at[3], s_wpair.at[0], partner).start()
     remote(bpart, bpair, s_send.at[4], s_wpair.at[1], partner).start()
 
-    hub_own[...] = dot(t_hub[...], gm[...])
+    def hub_part(rows):
+        hub_own[rows, :] = dot(t_hub[rows, :], gm[...])
+
+    in_blocks(hub_part, 2 * BIG)
     for y2 in range(rows_n // 2):
         pair_out[pl.ds(y2 * TILE, TILE), :] = hub_own[
             pl.ds(pl.multiple_of((y2 * 2 + 1 - core) * TILE, TILE), TILE), :
@@ -318,8 +367,10 @@
     )
     hub_recv[chip] = hub_send[chip]
 
-    gf_ref[...] = dot_cols(gp_ref[...], ws_ref[...])
-    gf_ref[...] += dot(t_loc[...], gm[...])
+    def local_back(rows):
+        gf_ref[rows, :] = dot_cols(gp_ref[rows, :], ws_ref[...]) + dot(t_loc[rows, :], gm[...])
+
+    in_blocks(local_back, 2 * BIG)
     drain(wrecv.at[pl.ds(0, chips - 1)], s_w)
     drain(brecv.at[pl.ds(0, chips - 1)], s_b)
     wown[...] = jnp.sum(wrecv[...].astype(F32), axis=0).astype(BF16)
@@ -333,7 +384,11 @@
 
     drain(recv2.at[pl.ds(0, total - 1)], s_gb)
 
-    gf_ref[...] += dot(t_list[...], recv2[...].reshape(total * bnd, width))
+
+    def return_part(rows):
+        gf_ref[rows, :] += dot(t_list[rows, :], recv2[...].reshape(total * bnd, width))
+
+    in_blocks(return_part, 2 * BIG)
     gf_copy = pltpu.make_async_copy(gf_ref, gf_out, s_io.at[3])
     gf_copy.start()
     drain(wrecv.at[pl.ds(0, chips - 1)], s_wag)
@@ -461,7 +516,7 @@
                 dma((12,)),
                 dma,
                 dma,
-                dma,
+                dma((rows_n // 2,)),
                 dma((2,)),
                 dma,
                 dma,

time: 78.9 us -> 76.4 us (0.968)
  Pallas kernels: 77.9 us -> 75.6 us
    pallas_call x1, Pallas kernels: 74.9 us -> 72.5 us  [body(): pl.pallas_call(functools.partial(kernel, rows_n, cols_n, fanouts), out_sh...]
where the time goes in v3:
time: 76.4 us; the launch traced here: 76.2 us
  Pallas kernels  75.6 us (99%)
    pallas_call x1, Pallas kernels, body(): pl.pallas_call(functools.partial(kernel, rows_n, cols_n, fanouts), out_sh...  72.5 us
    pallas_call x1, Pallas kernels, body(): pl.pallas_call(functools.partial(write_out, pieces), out_shape=tuple((jax...  3.05 us

profile of v3, /device:TPU:1, one launch (start us, length us, event | category | flops | bytes accessed | tf_op | source)
XLA Modules:
  0.0 76.2 jit_solution(12613198341237605236)
XLA Ops:
  0.6 72.5 %shard_map.145 = (bf16[2048,256]{1,0:T(8,128)(2,1)}, f32[2048,256]{1,0:T(8,128)}, f32[16,256]{1,0:T(8,128)}, f32[256,256]{1,0:T(8,128)}, f32[256,256]{1,0:T(8,128)}, /*index=5*/f32[1,256]{1,0:T(1,128)}) custom-call(bf16[2048,256]{1,0:T(8,128)(2,1)} %x_in.1, bf16[16,256]{1,0:T(8,128)(2,1)} %hub_ref.1, bf16[256,256]{1,0:T(8,128)(2,1)} %ws_ref.1, ...), custom_call_target="tpu_custom_call" | custom-call | tf_op jit(solution)/shard_map/pallas_call | solution.py:471
  73.2 3.0 %shard_map.146 = (bf16[2048,256]{1,0:T(8,128)(2,1)}, f32[2048,256]{1,0:T(8,128)}, f32[16,256]{1,0:T(8,128)}, f32[256,256]{1,0:T(8,128)}, f32[256,256]{1,0:T(8,128)}, /*index=5*/f32[1,256]{1,0:T(1,128)}) custom-call(bf16[2048,256]{1,0:T(8,128)(2,1)} %get-tuple-element.18.refs_0_, f32[2048,256]{1,0:T(8,128)} %get-tuple-element.19.refs_1_, ...), custom_call_target="tpu_custom_call" | custom-call | tf_op jit(solution)/shard_map/pallas_call | solution.py:546

commit v4 on v3

--- a/solution.py
+++ b/solution.py
@@ -19,6 +19,21 @@
     cols_n,
     fanouts,
     x_in,
+    hub_in,
+    ws_in,
+    wn_in,
+    bias_in,
+    el_in,
+    eh_in,
+    er_in,
+    es_in,
+    cot_in,
+    act_out,
+    gf_out,
+    ghub_ref,
+    gws_ref,
+    gwn_ref,
+    gb_ref,
     hub_ref,
     ws_ref,
     wn_ref,
@@ -27,13 +42,6 @@
     eh_ref,
     er_ref,
     es_ref,
-    cot_in,
-    act_out,
-    gf_out,
-    ghub_ref,
-    gws_ref,
-    gwn_ref,
-    gb_ref,
     x_ref,
     cot_ref,
     act_ref,
@@ -87,6 +95,23 @@
     x_copy.start()
     cot_copy = pltpu.make_async_copy(cot_in, cot_ref, s_io.at[1])
     cot_copy.start()
+    small = [
+        pltpu.make_async_copy(source, held, s_io.at[4 + k])
+        for k, (source, held) in enumerate(
+            (
+                (el_in, el_ref),
+                (eh_in, eh_ref),
+                (er_in, er_ref),
+                (es_in, es_ref),
+                (hub_in, hub_ref),
+                (ws_in, ws_ref),
+                (wn_in, wn_ref),
+                (bias_in, bias_ref),
+            )
+        )
+    ]
+    for copy in small:
+        copy.start()
     tiles = nodes // TILE
     bnd = send1.shape[1]
     row = lax.axis_index("row")
@@ -144,6 +169,8 @@
     for c2 in far_cols[:-1]:
         greet(row, c2)
 
+    for copy in small:
+        copy.wait()
     erow[...] = jnp.concatenate(
         [
             el_ref[...].astype(F32),
@@ -478,9 +505,17 @@
                 jax.ShapeDtypeStruct((width, width), F32),
                 jax.ShapeDtypeStruct((1, width), F32),
             ),
-            in_specs=[hbm] + [vmem] * 8 + [hbm],
+            in_specs=[hbm] * 10,
             out_specs=(hbm, hbm) + (vmem,) * 4,
             scratch_shapes=[
+                pltpu.VMEM((hub_own, width), BF16),
+                pltpu.VMEM((width, width), BF16),
+                pltpu.VMEM((width, width), BF16),
+                pltpu.VMEM((1, width), F32),
+                pltpu.VMEM((fanouts[0], nodes), jnp.int32),
+                pltpu.VMEM((fanouts[1], nodes), jnp.int32),
+                pltpu.VMEM((fanouts[2], nodes), jnp.int32),
+                pltpu.VMEM((1, send_rows.shape[1]), jnp.int32),
                 pltpu.VMEM((nodes, width), BF16),
                 pltpu.VMEM((nodes, width), BF16),
                 pltpu.VMEM((nodes, width), BF16),
@@ -525,7 +560,7 @@
                 dma,
                 dma,
                 dma,
-                dma((4,)),
+                dma((12,)),
             ],
             compiler_params=pltpu.CompilerParams(
                 collective_id=0, has_side_effects=True, vmem_limit_bytes=60 << 20

time: 76.4 us -> 75.7 us (level)
  no operation moved by 1% of the time
where the time goes in v4:
time: 75.7 us; the launch traced here: 75.5 us
  Pallas kernels  74.9 us (99%)
    pallas_call x1, Pallas kernels, body(): pl.pallas_call(functools.partial(kernel, rows_n, cols_n, fanouts), out_sh...  71.8 us
    pallas_call x1, Pallas kernels, body(): pl.pallas_call(functools.partial(write_out, pieces), out_shape=tuple((jax...  3.05 us

profile of v4, /device:TPU:1, one launch (start us, length us, event | category | flops | bytes accessed | tf_op | source)
XLA Modules:
  0.0 75.5 jit_solution(4158037118670571059)
XLA Ops:
  0.6 71.8 %shard_map.145 = (bf16[2048,256]{1,0:T(8,128)(2,1)}, f32[2048,256]{1,0:T(8,128)}, f32[16,256]{1,0:T(8,128)}, f32[256,256]{1,0:T(8,128)}, f32[256,256]{1,0:T(8,128)}, /*index=5*/f32[1,256]{1,0:T(1,128)}) custom-call(bf16[2048,256]{1,0:T(8,128)(2,1)} %x_in.1, bf16[16,256]{1,0:T(8,128)(2,1)} %hub_in.1, bf16[256,256]{1,0:T(8,128)(2,1)} %ws_in.1, ...), custom_call_target="tpu_custom_call" | custom-call | tf_op jit(solution)/shard_map/pallas_call | solution.py:498
  72.5 3.0 %shard_map.146 = (bf16[2048,256]{1,0:T(8,128)(2,1)}, f32[2048,256]{1,0:T(8,128)}, f32[16,256]{1,0:T(8,128)}, f32[256,256]{1,0:T(8,128)}, f32[256,256]{1,0:T(8,128)}, /*index=5*/f32[1,256]{1,0:T(1,128)}) custom-call(bf16[2048,256]{1,0:T(8,128)(2,1)} %get-tuple-element.18.refs_0_, f32[2048,256]{1,0:T(8,128)} %get-tuple-element.19.refs_1_, ...), custom_call_target="tpu_custom_call" | custom-call | tf_op jit(solution)/shard_map/pallas_call | solution.py:581

commit v5 on v4

--- a/solution.py
+++ b/solution.py
@@ -302,19 +302,14 @@
         pre = pre_ref[rows, :] + dot(mean, wn_ref[...])
         sig = jax.nn.sigmoid(pre)
         act_ref[rows, :] = (pre * sig).astype(BF16)
-        gp_ref[rows, :] = (
-            cot_ref[rows, :].astype(F32) * sig * (1.0 + pre * (1.0 - sig))
-        ).astype(BF16)
-
-    in_blocks(dense)
+        gp = (cot_ref[rows, :].astype(F32) * sig * (1.0 + pre * (1.0 - sig))).astype(BF16)
+        gp_ref[rows, :] = gp
+        gm[rows, :] = (dot_cols(gp, wn_ref[...]) / float(fanout)).astype(BF16)
+
+    in_blocks(dense, 2 * BIG)
     act_copy = pltpu.make_async_copy(act_ref, act_out, s_io.at[2])
     act_copy.start()
 
-
-    def back_mean(rows):
-        gm[rows, :] = (dot_cols(gp_ref[rows, :], wn_ref[...]) / float(fanout)).astype(BF16)
-
-    in_blocks(back_mean)
 
     def spread_and_send(i, c):
         y2 = lax.rem(yy + far(i), 4)

time: 75.7 us -> 74.9 us (0.989)
  Pallas kernels: 74.9 us -> 73.9 us
    pallas_call x1, Pallas kernels: 71.8 us -> 70.9 us  [body(): pl.pallas_call(functools.partial(kernel, rows_n, cols_n, fanouts), out_sh...]
where the time goes in v5:
time: 74.9 us; the launch traced here: 74.8 us
  Pallas kernels  73.9 us (99%)
  between operations  0.8 us (1%)
    pallas_call x1, Pallas kernels, body(): pl.pallas_call(functools.partial(kernel, rows_n, cols_n, fanouts), out_sh...  70.9 us
    pallas_call x1, Pallas kernels, body(): pl.pallas_call(functools.partial(write_out, pieces), out_shape=tuple((jax...  3.05 us

profile of v5, /device:TPU:1, one launch (start us, length us, event | category | flops | bytes accessed | tf_op | source)
XLA Modules:
  0.0 74.8 jit_solution(823806883138696362)
XLA Ops:
  0.6 70.9 %shard_map.145 = (bf16[2048,256]{1,0:T(8,128)(2,1)}, f32[2048,256]{1,0:T(8,128)}, f32[16,256]{1,0:T(8,128)}, f32[256,256]{1,0:T(8,128)}, f32[256,256]{1,0:T(8,128)}, /*index=5*/f32[1,256]{1,0:T(1,128)}) custom-call(bf16[2048,256]{1,0:T(8,128)(2,1)} %x_in.1, bf16[16,256]{1,0:T(8,128)(2,1)} %hub_in.1, bf16[256,256]{1,0:T(8,128)(2,1)} %ws_in.1, ...), custom_call_target="tpu_custom_call" | custom-call | tf_op jit(solution)/shard_map/pallas_call | solution.py:493
  71.5 3.0 %shard_map.146 = (bf16[2048,256]{1,0:T(8,128)(2,1)}, f32[2048,256]{1,0:T(8,128)}, f32[16,256]{1,0:T(8,128)}, f32[256,256]{1,0:T(8,128)}, f32[256,256]{1,0:T(8,128)}, /*index=5*/f32[1,256]{1,0:T(1,128)}) custom-call(bf16[2048,256]{1,0:T(8,128)(2,1)} %get-tuple-element.18.refs_0_, f32[2048,256]{1,0:T(8,128)} %get-tuple-element.19.refs_1_, ...), custom_call_target="tpu_custom_call" | custom-call | tf_op jit(solution)/shard_map/pallas_call | solution.py:576
